TPU v7x, 256 devices: a whole 4x4x8 slice. The times are simulated.
256 devices in a mesh: dp: 32 (over y, z), vocab: 8 (over x, core).
Axes of the slice: x: 4, y: 4, z: 8, core: 2. Of those that a mesh axis runs over, the one named last changes fastest.
Arguments:
- hidden: bfloat16 [24576, 2048], P('dp', 'vocab')
- gain: bfloat16 [2048], replicated, may hold values from 0.5 to 1.5
- head: bfloat16 [2048, 32000], P('dp', 'vocab')
- target_ids: int32 [24576], P('dp'), may hold values from 0 to 31999
- seq_lens: int32 [64], replicated, may hold values from 64 to 704, as said below
- seq_owner: int32 [64], replicated, may hold values from 0 to 31, as said below
Outputs:
- logprob: float32 [24576], P('dp')
- entropy: float32 [24576], P('dp')
Inputs may be any that keep to these rules, and one draw needn't show every extreme that they name: `seq_lens`: the lengths of the sequences owned by one dp index sum to at most 768; in every draw the sequences of some dp index sum to exactly 768. `seq_owner`: every dp index owns exactly 2 sequences.
All inputs are finite; a program needn't handle non-finite values.
Results may differ from a plain program's by a relative error of at most 0.0075.
Values may be sent and summed in bfloat16 or wider, within the bound.
A program may use at most 64 MiB of HBM per device.

v0:
```python
import jax
import jax.numpy as jnp
from jax import lax
from jax.sharding import PartitionSpec as P

EPS = 1e-05


def row_stats(normed, token_ids, columns, offset):
    count = normed.shape[0]
    width = normed.shape[1]
    block_rows = min(128, count)
    blocks = count // block_rows
    breadth = columns.shape[1]

    def compute(block_norm, block_ids):
        logits = jnp.dot(block_norm, columns, preferred_element_type=jnp.float32)
        top = jnp.max(logits, axis=1)
        expo = jnp.exp(logits - top[:, None])
        total = jnp.sum(expo, axis=1)
        weighted = jnp.sum(expo * logits, axis=1)
        local_id = block_ids - offset
        matches = jnp.arange(breadth, dtype=jnp.int32)[None, :] == local_id[:, None]
        picked = jnp.sum(jnp.where(matches, logits, 0.0), axis=1)
        return (top, total, weighted, picked)

    def per_block(item):
        block_norm, block_ids, start = item
        return compute(block_norm, block_ids)

    starts = jnp.arange(blocks, dtype=jnp.int32) * block_rows
    result = lax.map(
        per_block,
        (normed.reshape(blocks, block_rows, width), token_ids.reshape(blocks, block_rows), starts),
    )
    return tuple((member.reshape(count) for member in result))


def local(hidden, gain, head, target_ids, seq_lens, seq_owner):
    groups = lax.axis_size("dp")
    position = lax.axis_index("dp")
    slice_index = lax.axis_index("vocab")
    slots = hidden.shape[0]
    breadth = head.shape[1]
    owners = jnp.arange(groups, dtype=jnp.int32)
    loads = jnp.sum(jnp.where(seq_owner[:, None] == owners[None, :], seq_lens[:, None], 0), axis=0)
    own_live = jnp.arange(slots, dtype=jnp.int32) < loads[position]
    features = lax.all_gather(hidden, "vocab", axis=1, tiled=True)
    wide = features.astype(jnp.float32)
    normed = (
        wide
        * lax.rsqrt(jnp.mean(wide * wide, axis=1, keepdims=True) + EPS)
        * gain.astype(jnp.float32)
    ).astype(jnp.bfloat16)
    columns = lax.all_gather(head, "dp", axis=0, tiled=True)
    stats = row_stats(normed, target_ids, columns, slice_index * breadth)
    top = lax.pmax(stats[0], "vocab")
    factor = jnp.exp(stats[0] - top)
    total, weighted, picked = lax.psum((stats[1] * factor, stats[2] * factor, stats[3]), "vocab")
    lse = top + jnp.log(total)
    logprob = picked - lse
    entropy = lse - weighted / total
    return (jnp.where(own_live, logprob, 0.0), jnp.where(own_live, entropy, 0.0))


def solution(mesh):
    return jax.shard_map(
        local,
        mesh=mesh,
        in_specs=(P("dp", "vocab"), P(), P("dp", "vocab"), P("dp"), P(), P()),
        out_specs=(P("dp"), P("dp")),
        check_vma=False,
    )
```

profile of v0, /device:TPU:8, one launch (start us, length us, event | category | flops | bytes accessed | tf_op | source)
XLA Modules:
  0.0 306.3 jit_solution(14415921997200401669)
XLA Ops:
  7.2 0.7 all-gather.3.cloned.1.call-update
  7.9 0.7 all-gather.5.cloned.1.call-update
  8.7 0.7 convert_element_type.10
  9.4 0.8 select_reduce_fusion.1
  10.2 0.6 dynamic_slice.11
  10.8 36.1 %all-gather.3.cloned.1.call-done = bf16[768,2048]{1,0:T(8,128)(2,1)} async-done(((bf16[768,256]{1,0:T(8,128)(2,1)}), bf16[768,2048]{1,0:T(8,128)(2,1)}) %all-gather.3.cloned.1.call-update) | async-done | bytes 3145744 | tf_op jit(solution)/shard_map/all_gather | solution.py:48
  46.9 2.7 fusion.5
  49.6 0.1 copy-done
  49.7 2.5 fusion.7
  52.2 137.7 %all-gather.5.cloned.1.call-done = bf16[2048,4000]{1,0:T(8,128)(2,1)} async-done(((bf16[64,4000]{1,0:T(8,128)(2,1)}), bf16[2048,4000]{1,0:T(8,128)(2,1)}) %all-gather.5.cloned.1.call-update) | async-done | bytes 16384016 | tf_op jit(solution)/shard_map/all_gather | solution.py:55
  189.9 70.6 %while.16 = (s32[]{:T(128)}, f32[6,128]{1,0:T(8,128)S(1)}, f32[6,128]{1,0:T(8,128)S(1)}, f32[6,128]{1,0:T(8,128)S(1)}, f32[6,128]{1,0:T(8,128)S(1)}, /*index=5*/...) while((s32[]{:T(128)}, f32[6,128]{1,0:T(8,128)S(1)}, ...), condition=%wide.region_7.8_spmd, body=%wide.region_2.7_spmd.sunk | while | flops 2101247616 | bytes 21406340 | solution.py:32
  189.9 10.2 %fusion.13 = (f32[128]{0:T(128)S(1)}, f32[128,4000]{0,1:T(8,128)S(1)}) fusion(bf16[2048,4000]{1,0:T(8,128)(2,1)} %get-tuple-element.179, bf16[6,128,2048]{2,1,0:T(8,128)(2,1)} %get-tuple-element.178, s32[]{:T(128)} %get-tuple-element.162), kind=kOutput, calls=%fused_computation.25.clone.1 | convolution fusion | flops 2097663872 | bytes 19350528 | tf_op jit(solution)/shard_map/while/body/eval_jaxpr/dot_general | solution.py:17
  200.1 0.7 subtract_bitcast_fusion.2
  200.8 0.7 multiply_reduce_fusion.2
  201.6 10.2 %fusion.13 = (f32[128]{0:T(128)S(1)}, f32[128,4000]{0,1:T(8,128)S(1)}) fusion(bf16[2048,4000]{1,0:T(8,128)(2,1)} %get-tuple-element.179, bf16[6,128,2048]{2,1,0:T(8,128)(2,1)} %get-tuple-element.178, s32[]{:T(128)} %get-tuple-element.162), kind=kOutput, calls=%fused_computation.25.clone.1 | convolution fusion | flops 2097663872 | bytes 19350528 | tf_op jit(solution)/shard_map/while/body/eval_jaxpr/dot_general | solution.py:17
  211.9 0.7 subtract_bitcast_fusion.2
  212.6 0.7 multiply_reduce_fusion.2
  213.4 10.2 %fusion.13 = (f32[128]{0:T(128)S(1)}, f32[128,4000]{0,1:T(8,128)S(1)}) fusion(bf16[2048,4000]{1,0:T(8,128)(2,1)} %get-tuple-element.179, bf16[6,128,2048]{2,1,0:T(8,128)(2,1)} %get-tuple-element.178, s32[]{:T(128)} %get-tuple-element.162), kind=kOutput, calls=%fused_computation.25.clone.1 | convolution fusion | flops 2097663872 | bytes 19350528 | tf_op jit(solution)/shard_map/while/body/eval_jaxpr/dot_general | solution.py:17
  223.7 0.7 subtract_bitcast_fusion.2
  224.4 0.7 multiply_reduce_fusion.2
  225.2 10.2 %fusion.13 = (f32[128]{0:T(128)S(1)}, f32[128,4000]{0,1:T(8,128)S(1)}) fusion(bf16[2048,4000]{1,0:T(8,128)(2,1)} %get-tuple-element.179, bf16[6,128,2048]{2,1,0:T(8,128)(2,1)} %get-tuple-element.178, s32[]{:T(128)} %get-tuple-element.162), kind=kOutput, calls=%fused_computation.25.clone.1 | convolution fusion | flops 2097663872 | bytes 19350528 | tf_op jit(solution)/shard_map/while/body/eval_jaxpr/dot_general | solution.py:17
  235.4 0.7 subtract_bitcast_fusion.2
  236.1 0.7 multiply_reduce_fusion.2
  237.0 10.2 %fusion.13 = (f32[128]{0:T(128)S(1)}, f32[128,4000]{0,1:T(8,128)S(1)}) fusion(bf16[2048,4000]{1,0:T(8,128)(2,1)} %get-tuple-element.179, bf16[6,128,2048]{2,1,0:T(8,128)(2,1)} %get-tuple-element.178, s32[]{:T(128)} %get-tuple-element.162), kind=kOutput, calls=%fused_computation.25.clone.1 | convolution fusion | flops 2097663872 | bytes 19350528 | tf_op jit(solution)/shard_map/while/body/eval_jaxpr/dot_general | solution.py:17
  247.2 0.7 subtract_bitcast_fusion.2
  247.9 0.7 multiply_reduce_fusion.2
  248.7 10.2 %fusion.13 = (f32[128]{0:T(128)S(1)}, f32[128,4000]{0,1:T(8,128)S(1)}) fusion(bf16[2048,4000]{1,0:T(8,128)(2,1)} %get-tuple-element.179, bf16[6,128,2048]{2,1,0:T(8,128)(2,1)} %get-tuple-element.178, s32[]{:T(128)} %get-tuple-element.162), kind=kOutput, calls=%fused_computation.25.clone.1 | convolution fusion | flops 2097663872 | bytes 19350528 | tf_op jit(solution)/shard_map/while/body/eval_jaxpr/dot_general | solution.py:17
  259.0 0.7 subtract_bitcast_fusion.2
  259.7 0.7 multiply_reduce_fusion.2
  260.5 14.1 %pmax.7 = f32[768]{0:T(1024)S(1)} all-reduce(f32[768]{0:T(1024)S(1)} %bitcast.42), channel_id=1, replica_groups=mesh['dp'=32,'vocab'=8] {'vocab'}, use_global_device_ids=true, to_apply=%region_9.10 | all-reduce | flops 768 | bytes 6144 | tf_op jit(solution)/shard_map/pmax | solution.py:57
  274.7 23.6 %all-reduce = (f32[768]{0:T(1024)S(1)}, f32[768]{0:T(1024)S(1)}, f32[768]{0:T(1024)S(1)}) all-reduce(f32[768]{0:T(1024)S(1)} %bitcast.43, f32[768]{0:T(1024)S(1)} %get-tuple-element.85, f32[768]{0:T(1024)S(1)} %get-tuple-element.84), channel_id=1, replica_groups=mesh['dp'=32,'vocab'=8] {'vocab'}, use_global_device_ids=true, to_apply=%region_8.9 | all-reduce | flops 2304 | bytes 18432 | tf_op jit(solution)/shard_map/psum | solution.py:59
  298.2 1.2 subtract_select_fusion
  (33 shorter events, 0.9 us)
Async XLA Ops:
  7.2 39.7 %all-gather.3.cloned.1.call-start = ((), (), s32[]{:S(2)}) async-start(), calls=%async_computation | async-start | bytes 3538944 | tf_op jit(solution)/shard_map/all_gather | solution.py:48
  7.9 182.0 %all-gather.5.cloned.1.call-start = ((), (), s32[]{:S(2)}) async-start(), calls=%async_computation.1 | async-start | bytes 17301504 | tf_op jit(solution)/shard_map/all_gather | solution.py:55
  46.9 2.8 copy-start
Sparse Core Ops, SparseCore 0:
  9.8 37.0 all-gather.2
  49.5 140.3 all-gather.4
where the time goes:
time: 307 us; the launch traced here: 306 us
  waiting for transfers between devices  175 us (57%)
  matrix products  61.4 us (20%)
  blocking collectives  37.7 us (12%)
  other arithmetic  16.2 us (5%)
  between operations  14.1 us (5%)
    all_gather x1, waiting for transfers between devices, local(): columns = lax.all_gather(head, 'dp', axis=0, tiled=True)  138 us
    dot_general x6, matrix products, compute(): logits = jnp.dot(block_norm, columns, preferred_element_type=jnp.float32)  61.4 us
    all_gather x1, waiting for transfers between devices, local(): features = lax.all_gather(hidden, 'vocab', axis=1, tiled=True)  36.1 us
    psum x1, blocking collectives, local(): lax.psum((stats[1] * factor, stats[2] * factor, stats[3]), 'vocab')  23.6 us
    pmax x1, blocking collectives, local(): top = lax.pmax(stats[0], 'vocab')  14.1 us
  transfers between devices with their start and end apart: 2, of which 2 were waited for; matrix products, arithmetic and copies ran while one was open for 2% of the time, Pallas kernels for 0%

commit v1 on v0

--- a/solution.py
+++ b/solution.py
@@ -4,6 +4,13 @@
 from jax.sharding import PartitionSpec as P
 
 EPS = 1e-05
+
+
+def gather_over(x, axis, dim):
+    size = lax.axis_size(axis)
+    blocks = jnp.stack([x for _ in range(size)])
+    blocks = lax.all_to_all(blocks, axis, split_axis=0, concat_axis=0)
+    return jnp.concatenate(blocks, axis=dim)
 
 
 def row_stats(normed, token_ids, columns, offset):
@@ -45,7 +52,7 @@
     owners = jnp.arange(groups, dtype=jnp.int32)
     loads = jnp.sum(jnp.where(seq_owner[:, None] == owners[None, :], seq_lens[:, None], 0), axis=0)
     own_live = jnp.arange(slots, dtype=jnp.int32) < loads[position]
-    features = lax.all_gather(hidden, "vocab", axis=1, tiled=True)
+    features = gather_over(hidden, "vocab", 1)
     wide = features.astype(jnp.float32)
     normed = (
         wide

time: 307 us -> 270 us (0.88)
  waiting for transfers between devices: 175 us -> 117 us
  local copies, waits for them, and re-layouts: 1.51 us -> 17.7 us
  starting transfers between devices: 0.08 us -> 4.47 us
    all_gather x1, waiting for transfers between devices: 138 us -> 79.2 us  [local(): columns = lax.all_gather(head, 'dp', axis=0, tiled=True)]
    all_to_all x0 -> x1, waiting for transfers between devices: none -> 37.6 us  [gather_over(): blocks = lax.all_to_all(blocks, axis, split_axis=0, concat_axis=0)]
    all_gather x1 -> x0, waiting for transfers between devices: 36.1 us -> none  [local(): features = lax.all_gather(hidden, 'vocab', axis=1, tiled=True)]
    convert_element_type x0 -> x2, local copies, waits for them, and re-layouts: none -> 13.4 us  [local(): wide = features.astype(jnp.float32)]
    all_to_all x0 -> x1, starting transfers between devices: none -> 4.43 us  [gather_over(): blocks = lax.all_to_all(blocks, axis, split_axis=0, concat_axis=0)]
  transfers between devices with their start and end apart: 2 -> 2, of which waited for: 2 -> 2; matrix products, arithmetic and copies ran while one was open for 2% -> 9% of each run, Pallas kernels for 0% -> 0%
where the time goes in v1:
time: 270 us; the launch traced here: 269 us
  waiting for transfers between devices  117 us (43%)
  matrix products  61.4 us (23%)
  blocking collectives  37.7 us (14%)
  local copies, waits for them, and re-layouts  17.7 us (7%)
  other arithmetic  16.2 us (6%)
  between operations  14.1 us (5%)
  starting transfers between devices  4.47 us (2%)
    all_gather x1, waiting for transfers between devices, local(): columns = lax.all_gather(head, 'dp', axis=0, tiled=True)  79.2 us
    dot_general x6, matrix products, compute(): logits = jnp.dot(block_norm, columns, preferred_element_type=jnp.float32)  61.4 us
    all_to_all x1, waiting for transfers between devices, gather_over(): blocks = lax.all_to_all(blocks, axis, split_axis=0, concat_axis=0)  37.6 us
    psum x1, blocking collectives, local(): lax.psum((stats[1] * factor, stats[2] * factor, stats[3]), 'vocab')  23.6 us
    pmax x1, blocking collectives, local(): top = lax.pmax(stats[0], 'vocab')  14.1 us
    convert_element_type x2, local copies, waits for them, and re-layouts, local(): wide = features.astype(jnp.float32)  13.4 us
  transfers between devices with their start and end apart: 2, of which 2 were waited for; matrix products, arithmetic and copies ran while one was open for 9% of the time, Pallas kernels for 0%

profile of v1, /device:TPU:8, one launch (start us, length us, event | category | flops | bytes accessed | tf_op | source)
XLA Modules:
  0.0 269.3 jit_solution(14433939102058908429)
XLA Ops:
  7.2 0.7 all-gather.2.cloned.1.call-update
  7.9 2.9 %stack.2 = bf16[8,768,256]{2,1,0:T(8,128)(2,1)} broadcast(bf16[768,256]{1,0:T(8,128)(2,1)} %param.8), dimensions={1,2} | broadcast | bytes 3538944 | tf_op jit(solution)/shard_map/stack | solution.py:11
  10.8 4.4 %all-to-all-start = ((bf16[8,768,256]{2,1,0:T(8,128)(2,1)}), bf16[8,768,256]{2,1,0:T(8,128)(2,1)S(1)}, u32[]{:S(2)}, u32[]{:S(2)}) async-start(bf16[8,768,256]{2,1,0:T(8,128)(2,1)} %stack.2), calls=%async_computation | async-start | bytes 6291456 | tf_op jit(solution)/shard_map/all_to_all | solution.py:12
  15.4 0.7 dynamic_slice.11
  16.0 37.6 %all-to-all-done = bf16[8,768,256]{2,1,0:T(8,128)(2,1)S(1)} async-done(((bf16[8,768,256]{2,1,0:T(8,128)(2,1)}), bf16[8,768,256]{2,1,0:T(8,128)(2,1)S(1)}, u32[]{:S(2)}, u32[]{:S(2)}) %all-to-all-start) | async-done | bytes 3145760 | tf_op jit(solution)/shard_map/all_to_all | solution.py:12
  54.2 6.3 %copy.9 = f32[768,8,256]{2,1,0:T(8,128)} copy(f32[768,8,256]{2,0,1:T(8,128)S(1)} %convert_bitcast_fusion) | data formatting | bytes 12582912 | tf_op jit(solution)/shard_map/convert_element_type | solution.py:56
  60.5 7.1 %reshape.67 = f32[6,128,2048]{2,1,0:T(8,128)} reshape(f32[768,8,256]{2,1,0:T(8,128)} %copy.9) | data formatting | bytes 12582912 | tf_op jit(solution)/shard_map/convert_element_type | solution.py:56
  67.6 0.7 fusion.5
  68.3 5.3 %multiply_convert_fusion = bf16[6,128,2048]{2,1,0:T(8,128)(2,1)} fusion(f32[6,128,2048]{2,1,0:T(8,128)} %reshape.67, f32[2048]{0:T(1024)S(1)} %convert_element_type.25, f32[6,128]{1,0:T(8,128)S(1)} %rsqrt_bitcast_fusion), kind=kLoop, calls=%fused_computation.13 | loop fusion | flops 4718592 | bytes 9448448 | tf_op jit(solution)/shard_map/convert_element_type | solution.py:61
  73.6 79.2 %all-gather.2.cloned.1.call-done = bf16[2048,4000]{1,0:T(8,128)(2,1)} async-done(((bf16[64,4000]{1,0:T(8,128)(2,1)}), bf16[2048,4000]{1,0:T(8,128)(2,1)}) %all-gather.2.cloned.1.call-update) | async-done | bytes 16384016 | tf_op jit(solution)/shard_map/all_gather | solution.py:62
  152.8 70.6 %while.16 = (s32[]{:T(128)}, f32[6,128]{1,0:T(8,128)S(1)}, f32[6,128]{1,0:T(8,128)S(1)}, f32[6,128]{1,0:T(8,128)S(1)}, f32[6,128]{1,0:T(8,128)S(1)}, /*index=5*/...) while((s32[]{:T(128)}, f32[6,128]{1,0:T(8,128)S(1)}, ...), condition=%wide.region_7.8_spmd, body=%wide.region_2.7_spmd.sunk | while | flops 2101247616 | bytes 21406340 | solution.py:39
  152.8 10.2 %fusion.11 = (f32[128]{0:T(128)S(1)}, f32[128,4000]{0,1:T(8,128)S(1)}) fusion(bf16[2048,4000]{1,0:T(8,128)(2,1)} %get-tuple-element.179, bf16[6,128,2048]{2,1,0:T(8,128)(2,1)} %get-tuple-element.178, s32[]{:T(128)} %get-tuple-element.162), kind=kOutput, calls=%fused_computation.24.clone.1 | convolution fusion | flops 2097663872 | bytes 19350528 | tf_op jit(solution)/shard_map/while/body/eval_jaxpr/dot_general | solution.py:24
  163.0 0.7 subtract_bitcast_fusion.2
  163.7 0.7 multiply_reduce_fusion.2
  164.6 10.2 %fusion.11 = (f32[128]{0:T(128)S(1)}, f32[128,4000]{0,1:T(8,128)S(1)}) fusion(bf16[2048,4000]{1,0:T(8,128)(2,1)} %get-tuple-element.179, bf16[6,128,2048]{2,1,0:T(8,128)(2,1)} %get-tuple-element.178, s32[]{:T(128)} %get-tuple-element.162), kind=kOutput, calls=%fused_computation.24.clone.1 | convolution fusion | flops 2097663872 | bytes 19350528 | tf_op jit(solution)/shard_map/while/body/eval_jaxpr/dot_general | solution.py:24
  174.8 0.7 subtract_bitcast_fusion.2
  175.5 0.7 multiply_reduce_fusion.2
  176.4 10.2 %fusion.11 = (f32[128]{0:T(128)S(1)}, f32[128,4000]{0,1:T(8,128)S(1)}) fusion(bf16[2048,4000]{1,0:T(8,128)(2,1)} %get-tuple-element.179, bf16[6,128,2048]{2,1,0:T(8,128)(2,1)} %get-tuple-element.178, s32[]{:T(128)} %get-tuple-element.162), kind=kOutput, calls=%fused_computation.24.clone.1 | convolution fusion | flops 2097663872 | bytes 19350528 | tf_op jit(solution)/shard_map/while/body/eval_jaxpr/dot_general | solution.py:24
  186.6 0.7 subtract_bitcast_fusion.2
  187.3 0.7 multiply_reduce_fusion.2
  188.1 10.2 %fusion.11 = (f32[128]{0:T(128)S(1)}, f32[128,4000]{0,1:T(8,128)S(1)}) fusion(bf16[2048,4000]{1,0:T(8,128)(2,1)} %get-tuple-element.179, bf16[6,128,2048]{2,1,0:T(8,128)(2,1)} %get-tuple-element.178, s32[]{:T(128)} %get-tuple-element.162), kind=kOutput, calls=%fused_computation.24.clone.1 | convolution fusion | flops 2097663872 | bytes 19350528 | tf_op jit(solution)/shard_map/while/body/eval_jaxpr/dot_general | solution.py:24
  198.4 0.7 subtract_bitcast_fusion.2
  199.1 0.7 multiply_reduce_fusion.2
  199.9 10.2 %fusion.11 = (f32[128]{0:T(128)S(1)}, f32[128,4000]{0,1:T(8,128)S(1)}) fusion(bf16[2048,4000]{1,0:T(8,128)(2,1)} %get-tuple-element.179, bf16[6,128,2048]{2,1,0:T(8,128)(2,1)} %get-tuple-element.178, s32[]{:T(128)} %get-tuple-element.162), kind=kOutput, calls=%fused_computation.24.clone.1 | convolution fusion | flops 2097663872 | bytes 19350528 | tf_op jit(solution)/shard_map/while/body/eval_jaxpr/dot_general | solution.py:24
  210.2 0.7 subtract_bitcast_fusion.2
  210.9 0.7 multiply_reduce_fusion.2
  211.7 10.2 %fusion.11 = (f32[128]{0:T(128)S(1)}, f32[128,4000]{0,1:T(8,128)S(1)}) fusion(bf16[2048,4000]{1,0:T(8,128)(2,1)} %get-tuple-element.179, bf16[6,128,2048]{2,1,0:T(8,128)(2,1)} %get-tuple-element.178, s32[]{:T(128)} %get-tuple-element.162), kind=kOutput, calls=%fused_computation.24.clone.1 | convolution fusion | flops 2097663872 | bytes 19350528 | tf_op jit(solution)/shard_map/while/body/eval_jaxpr/dot_general | solution.py:24
  221.9 0.7 subtract_bitcast_fusion.2
  222.6 0.7 multiply_reduce_fusion.2
  223.5 14.1 %pmax.7 = f32[768]{0:T(1024)S(1)} all-reduce(f32[768]{0:T(1024)S(1)} %bitcast.44), channel_id=1, replica_groups=mesh['dp'=32,'vocab'=8] {'vocab'}, use_global_device_ids=true, to_apply=%region_9.10 | all-reduce | flops 768 | bytes 6144 | tf_op jit(solution)/shard_map/pmax | solution.py:64
  237.6 23.6 %all-reduce = (f32[768]{0:T(1024)S(1)}, f32[768]{0:T(1024)S(1)}, f32[768]{0:T(1024)S(1)}) all-reduce(f32[768]{0:T(1024)S(1)} %bitcast.45, f32[768]{0:T(1024)S(1)} %get-tuple-element.85, f32[768]{0:T(1024)S(1)} %get-tuple-element.84), channel_id=1, replica_groups=mesh['dp'=32,'vocab'=8] {'vocab'}, use_global_device_ids=true, to_apply=%region_8.9 | all-reduce | flops 2304 | bytes 18432 | tf_op jit(solution)/shard_map/psum | solution.py:66
  261.2 1.3 subtract_select_fusion
  (40 shorter events, 1.6 us)
Async XLA Ops:
  7.2 145.7 %all-gather.2.cloned.1.call-start = ((), (), s32[]{:S(2)}) async-start(), calls=%async_computation.1 | async-start | bytes 17301504 | tf_op jit(solution)/shard_map/all_gather | solution.py:62
  10.8 4.5 %copy-start = (bf16[2048]{0:T(1024)(128)(2,1)S(1)}, bf16[2048]{0:T(1024)(128)(2,1)}, u32[]{:S(2)}) copy-start(bf16[2048]{0:T(1024)(128)(2,1)} %param.9) | copy-start | bytes 12292
  10.8 4.5 %copy-start.1 = (s32[64]{0:T(128)S(1)}, s32[64]{0:T(128)}, u32[]{:S(2)}) copy-start(s32[64]{0:T(128)} %param.12) | copy-start | bytes 772
  10.8 4.5 %copy-start.2 = (s32[64]{0:T(128)S(1)}, s32[64]{0:T(128)}, u32[]{:S(2)}) copy-start(s32[64]{0:T(128)} %param.13) | copy-start | bytes 772
  10.8 42.9 %all-to-all-start = ((bf16[8,768,256]{2,1,0:T(8,128)(2,1)}), bf16[8,768,256]{2,1,0:T(8,128)(2,1)S(1)}, u32[]{:S(2)}, u32[]{:S(2)}) async-start(bf16[8,768,256]{2,1,0:T(8,128)(2,1)} %stack.2), calls=%async_computation | async-start | bytes 6291456 | tf_op jit(solution)/shard_map/all_to_all | solution.py:12
Sparse Core Ops, SparseCore 0:
  10.6 142.1 all-gather.1
